TPU v7x, 512 devices: a whole 4x4x16 slice. The times are simulated.
512 devices in a mesh: ktot: 32 (over z_lo, y, core), kvir: 16 (over z_hi, x).
Axes of the slice: x: 4, y: 4, z: 16 (z_hi: 4, z_lo: 4; z = z_hi * 4 + z_lo), core: 2. Of those that a mesh axis runs over, the one named last changes fastest.
Arguments:
- amplitudes: bfloat16 [32, 16, 672, 1024], P('ktot', 'kvir'), may hold values from -6 to 6
- ladder_integrals: bfloat16 [32, 16, 1024, 1024], P('ktot', 'kvir'), may hold values from -0.046875 to 0.046875
- listed: int32 [32, 16], P('ktot', 'kvir'), may hold values 0 or 1
- current: bfloat16 [32, 672, 1024], P('ktot', 'kvir'), may hold values from -3 to 3
- denominators: float32 [32, 672, 1024], P('ktot', 'kvir'), may hold values from 2 to 8
- cycle_integrals: bfloat16 [32, 512, 512], P('ktot', 'kvir'), may hold values from -0.25 to 0.25
Outputs:
- ladder_res: bfloat16 [32, 672, 1024], P('ktot', 'kvir')
- cycle_res: float32 [32, 1344, 1344], P('ktot', 'kvir')
All inputs are finite; a program needn't handle non-finite values. No bound on the sum of `listed` on one device may be relied on, other than what follows from the above.
Results may differ from a plain program's by a relative error of at most 0.017.
Values may be sent and summed in bfloat16 or wider, within the bound.
No kernel may reach another device: no remote copies, remote signals or barrier semaphores. Data moves between devices by JAX's collectives and lax.ppermute only.
A program may use at most 64 MiB of HBM per device.

v0:
```python
import jax
import jax.numpy as jnp
from jax import lax
from jax.experimental import pallas as pl
from jax.experimental.pallas import tpu as pltpu
from jax.sharding import Mesh, PartitionSpec as P


KTOT = ("zl", "y", "core")
KVIR = ("zh", "x")
SIZES = (4, 4, 2, 4, 4)
INTERPRET = False
BLOCK = 512
WHOLE = pl.BlockSpec(memory_space=pltpu.VMEM)


def near(array):
    return array if INTERPRET else pltpu.with_memory_space_constraint(array, pltpu.VMEM)


def near_out(shape):
    return jax.ShapeDtypeStruct(shape, jnp.bfloat16) if INTERPRET else pltpu.VMEM(shape, jnp.bfloat16)


def exchange(blocks, axis):
    return lax.all_to_all(blocks, axis, split_axis=0, concat_axis=0, tiled=True)


def steps(block, axis):
    count = lax.axis_size(axis)
    pieces = [block]
    for step in range(1, count):
        ring = [(i, (i + step) % count) for i in range(count)]
        pieces.append(lax.ppermute(block, axis, ring))
    return pieces


def ordered(pieces, axis):
    count = len(pieces)
    me = lax.axis_index(axis)
    stacked = jnp.stack(pieces)
    return jnp.stack([lax.dynamic_index_in_dim(stacked, (me - p) % count, 0, False) for p in range(count)])


def columns_block(width):
    return BLOCK if width % BLOCK == 0 else width


def ladder_part(amp, weights, listed, nz, nx):
    rows, inner = amp.shape
    width = weights.shape[1]
    one = rows // (nz * nx)
    tn = columns_block(width)

    def kernel(mark_ref, amp_ref, w_ref, out_ref):
        product = jnp.dot(amp_ref[...], w_ref[...], preferred_element_type=jnp.float32)
        product = product * mark_ref[...].astype(jnp.float32)
        here = pl.ds(pl.multiple_of(pl.program_id(0) * tn, tn), tn)
        for x in range(nx):
            slabs = [product[(z * nx + x) * one : (z * nx + x + 1) * one] for z in range(nz)]
            out_ref[x, :, here] = jnp.concatenate(slabs, 0).astype(jnp.bfloat16)

    return pl.pallas_call(
        kernel,
        grid=(width // tn,),
        in_specs=[
            pl.BlockSpec((1, 1), lambda j: (0, 0)),
            pl.BlockSpec((rows, inner), lambda j: (0, 0)),
            pl.BlockSpec((inner, tn), lambda j: (0, j)),
        ],
        out_specs=WHOLE,
        out_shape=near_out((nx, nz * one, width)),
        interpret=INTERPRET,
        name="ladder_part",
    )(listed, amp, weights)


def sum_over_x(got, nz):
    nx, rows, width = got.shape
    one = rows // nz
    tn = columns_block(width)

    def kernel(in_ref, out_ref):
        for j in range(width // tn):
            here = slice(j * tn, (j + 1) * tn)
            total = in_ref[0, :, here].astype(jnp.float32)
            for x in range(1, nx):
                total = total + in_ref[x, :, here].astype(jnp.float32)
            for z in range(nz):
                out_ref[z, :, here] = total[z * one : (z + 1) * one].astype(jnp.bfloat16)

    return pl.pallas_call(
        kernel,
        in_specs=[WHOLE],
        out_specs=WHOLE,
        out_shape=near_out((nz, one, width)),
        interpret=INTERPRET,
        name="sum_over_x",
    )(near(got))


def update(got, current, denominators):
    nz, one, width = got.shape

    def kernel(in_ref, current_ref, den_ref, ladder_ref, updated_ref):
        total = in_ref[0].astype(jnp.float32)
        for z in range(1, nz):
            total = total + in_ref[z].astype(jnp.float32)
        ladder_ref[...] = total.astype(jnp.bfloat16)
        updated_ref[...] = (current_ref[...].astype(jnp.float32) + total / den_ref[...]).astype(jnp.bfloat16)

    return pl.pallas_call(
        kernel,
        in_specs=[WHOLE] * 3,
        out_specs=[WHOLE] * 2,
        out_shape=[jax.ShapeDtypeStruct((one, width), jnp.bfloat16), near_out((one, width))],
        interpret=INTERPRET,
        name="update",
    )(near(got), current, denominators)


def step(amplitudes, ladder_integrals, listed, current, denominators, cycle_integrals):
    nx = lax.axis_size("x")
    nz = lax.axis_size("zh")
    rows_dev, width = current.shape[1:]
    tot_count = lax.axis_size(KTOT)
    col_width = width // tot_count

    cols = cycle_integrals.shape[2]

    part = ladder_part(amplitudes[0, 0], ladder_integrals[0, 0], listed, nz, nx)
    part, own = lax.optimization_barrier((part, cycle_integrals[0]))
    got = exchange(part, "x")
    own = own.reshape(col_width, nz, nx, col_width).transpose(0, 2, 1, 3).reshape(col_width, cols)
    own_pieces = steps(own, "zh")
    part = sum_over_x(got, nz)
    got = exchange(part, "zh")
    ints = ordered(own_pieces, "zh").reshape(nz * col_width, cols)
    int_pieces = steps(ints, "x")
    ladder, updated = update(got, current[0], denominators[0])

    received = lax.all_to_all(
        updated.reshape(rows_dev, tot_count, col_width), KTOT, split_axis=1, concat_axis=1, tiled=True
    )
    local = received.transpose(2, 0, 1).reshape(col_width, rows_dev * tot_count)
    cycle = lax.all_gather(local, "zh", axis=0).reshape(nz * col_width, -1)
    cycle_rows = cycle.shape[1]
    share = cycle_rows // (nx * nz)
    start = lax.axis_index(KVIR) * share
    first = (((0,), (0,)), ((), ()))
    pieces = steps(cycle, "x")
    mixed = 0.0
    for piece, weight in zip(pieces, int_pieces):
        mine = lax.dynamic_slice_in_dim(piece, start, share, 1)
        mixed += lax.dot_general(mine, weight, first, preferred_element_type=jnp.float32)
    mixed = mixed.astype(jnp.bfloat16)
    out = 0.0
    wide = nz * col_width
    me = lax.axis_index("x")
    for step, piece in enumerate(pieces):
        left = lax.dynamic_slice_in_dim(mixed, ((me - step) % nx) * wide, wide, 1)
        out += jnp.dot(left, piece, preferred_element_type=jnp.float32)
    return (ladder[None], (out * cols ** (-0.5))[None])


def solution(mesh):
    fine = Mesh(mesh.devices.reshape(SIZES), KTOT + KVIR)
    block = P(KTOT, KVIR, None)
    return jax.shard_map(
        step,
        mesh=fine,
        in_specs=(
            P(KTOT, KVIR, None, None),
            P(KTOT, KVIR, None, None),
            P(KTOT, KVIR),
            block,
            block,
            block,
        ),
        out_specs=(block, block),
        check_vma=False,
    )
```

profile of v0, /device:TPU:102, one launch (start us, length us, event | category | flops | bytes accessed | tf_op | source)
XLA Modules:
  0.0 157.4 jit_solution(17758925682523320171)
XLA Ops:
  1.3 3.5 %ladder_part.1 = bf16[4,168,1024]{2,1,0:T(8,128)(2,1)S(1)} custom-call(s32[1,1]{1,0:T(1,128)S(6)} %copy.25.mark_ref, bf16[672,1024]{1,0:T(8,128)(2,1)} %bitcast.38, bf16[1024,1024]{1,0:T(8,128)(2,1)} %bitcast.32), custom_call_target="tpu_custom_call" | custom-call | tf_op jit(solution)/shard_map/ladder_part/pallas_call | solution.py:63
  4.8 21.1 %all_to_all.15.in_ref = bf16[4,168,1024]{2,1,0:T(8,128)(2,1)S(1)} all-to-all(bf16[4,168,1024]{2,1,0:T(8,128)(2,1)S(1)} %ladder_part.1), channel_id=1, replica_groups=mesh['zl'=4,'y'=4,'core'=2,'zh'=4,'x'=4] {'x'}, dimensions={0} | all-to-all | bytes 2752512 | tf_op jit(solution)/shard_map/all_to_all | solution.py:26
  25.9 1.0 sum_over_x.1
  26.8 12.5 %all-to-all-start.1 = ((bf16[4,42,1024]{2,1,0:T(8,128)(2,1)}), bf16[4,42,1024]{2,1,0:T(8,128)(2,1)S(1)}, u32[]{:S(2)}, u32[]{:S(2)}) async-start(bf16[4,42,1024]{2,1,0:T(8,128)(2,1)} %sum_over_x.1), calls=%async_computation.1 | async-start | bytes 786432 | tf_op jit(solution)/shard_map/all_to_all | solution.py:26
  39.3 0.0 copy-done
  39.3 0.7 copy.23
  40.0 18.9 %all-to-all-done.1.in_ref = bf16[4,42,1024]{2,1,0:T(8,128)(2,1)S(1)} async-done(((bf16[4,42,1024]{2,1,0:T(8,128)(2,1)}), bf16[4,42,1024]{2,1,0:T(8,128)(2,1)S(1)}, u32[]{:S(2)}, u32[]{:S(2)}) %all-to-all-start.1) | async-done | bytes 344096 | tf_op jit(solution)/shard_map/all_to_all | solution.py:26
  58.9 1.7 %update.1 = (bf16[42,1024]{1,0:T(8,128)(2,1)}, bf16[42,1024]{1,0:T(8,128)(2,1)S(1)}) custom-call(bf16[4,42,1024]{2,1,0:T(8,128)(2,1)S(1)} %all-to-all-done.1.in_ref, bf16[42,1024]{1,0:T(8,128)(2,1)} %bitcast.47, f32[42,1024]{1,0:T(8,128)} %bitcast.42), custom_call_target="tpu_custom_call" | custom-call | tf_op jit(solution)/shard_map/update/pallas_call | solution.py:112
  60.6 0.2 copy.19
  60.8 1.0 reshape.24
  61.8 12.3 %all-to-all-start.2 = ((bf16[32,2,672]{2,1,0:T(2,128)(2,1)}), bf16[32,2,672]{2,1,0:T(2,128)(2,1)S(1)}, u32[]{:S(2)}, u32[]{:S(2)}) async-start(bf16[32,2,672]{2,1,0:T(2,128)(2,1)} %reshape.24), calls=%async_computation.2 | async-start | bytes 196608 | tf_op jit(solution)/shard_map/all_to_all | solution.py:142
  74.1 0.0 copy-done.1
  74.1 0.1 reshape.21
  74.2 0.1 copy.24
  74.3 0.2 reshape.22
  74.4 5.0 %collective-permute-start.2 = (bf16[32,512]{1,0:T(8,128)(2,1)S(1)}, bf16[32,512]{1,0:T(8,128)(2,1)S(1)}, u32[]{:S(2)}, u32[]{:S(2)}) collective-permute-start(bf16[32,512]{1,0:T(8,128)(2,1)S(1)} %reshape.22), channel_id=1, source_target_pairs={{0,12},{4,0},{8,4},{12,8},{1,13},{5,1},{9,5},{13,9},{2,14},{6,2},{... | collective-permute-start | bytes 98312 | tf_op jit(solution)/shard_map/ppermute | solution.py:34
  79.5 5.9 %collective-permute-start.1 = (bf16[32,512]{1,0:T(8,128)(2,1)S(1)}, bf16[32,512]{1,0:T(8,128)(2,1)S(1)}, u32[]{:S(2)}, u32[]{:S(2)}) collective-permute-start(bf16[32,512]{1,0:T(8,128)(2,1)S(1)} %reshape.22), channel_id=1, source_target_pairs={{0,8},{4,12},{8,0},{12,4},{1,9},{5,13},{9,1},{13,5},{2,10},{6,14},... | collective-permute-start | bytes 98312 | tf_op jit(solution)/shard_map/ppermute | solution.py:34
  85.4 3.8 %collective-permute-start = (bf16[32,512]{1,0:T(8,128)(2,1)S(1)}, bf16[32,512]{1,0:T(8,128)(2,1)S(1)}, u32[]{:S(2)}, u32[]{:S(2)}) collective-permute-start(bf16[32,512]{1,0:T(8,128)(2,1)S(1)} %reshape.22), channel_id=1, source_target_pairs={{0,4},{4,8},{8,12},{12,0},{1,5},{5,9},{9,13},{13,1},{2,6},{6,10},{... | collective-permute-start | bytes 98312 | tf_op jit(solution)/shard_map/ppermute | solution.py:34
  89.2 0.2 stack_reshape.3
  89.5 0.0 collective-permute-done.2
  89.5 4.4 %collective-permute-done.1 = bf16[32,512]{1,0:T(8,128)(2,1)S(1)} collective-permute-done((bf16[32,512]{1,0:T(8,128)(2,1)S(1)}, bf16[32,512]{1,0:T(8,128)(2,1)S(1)}, u32[]{:S(2)}, u32[]{:S(2)}) %collective-permute-start.1) | collective-permute-done | bytes 32800 | tf_op jit(solution)/shard_map/ppermute | solution.py:34
  94.0 3.2 %collective-permute-done = bf16[32,512]{1,0:T(8,128)(2,1)S(1)} collective-permute-done((bf16[32,512]{1,0:T(8,128)(2,1)S(1)}, bf16[32,512]{1,0:T(8,128)(2,1)S(1)}, u32[]{:S(2)}, u32[]{:S(2)}) %collective-permute-start) | collective-permute-done | bytes 32800 | tf_op jit(solution)/shard_map/ppermute | solution.py:34
  97.2 0.0 all-to-all-done.2
  97.3 0.4 reshape.25
  97.7 0.4 copy.16
  98.1 0.3 all_gather_reshape.3
  98.4 21.8 %all_gather.3 = bf16[4,32,1344]{2,1,0:T(8,128)(2,1)S(1)} all-gather(bf16[1,32,1344]{2,1,0:T(8,128)(2,1)S(1)} %all_gather_reshape.3), channel_id=1, replica_groups=mesh['zl'=4,'y'=4,'core'=2,'zh'=4,'x'=4] {'zh'}, dimensions={0}, use_global_device_ids=true | all-gather | bytes 430080 | tf_op jit(solution)/shard_map/all_gather | solution.py:146
  120.2 4.0 %collective-permute-start.3 = (bf16[128,1344]{1,0:T(8,128)(2,1)S(1)}, bf16[128,1344]{1,0:T(8,128)(2,1)S(1)}, u32[]{:S(2)}, u32[]{:S(2)}) collective-permute-start(bf16[128,1344]{1,0:T(8,128)(2,1)S(1)} %bitcast.33), channel_id=1, source_target_pairs={{0,1},{1,2},{2,3},{3,0},{4,5},{5,6},{6,7},{7,4},{8,9},{9,10},{10,1... | collective-permute-start | bytes 1032200 | tf_op jit(solution)/shard_map/ppermute | solution.py:34
  124.2 1.9 %collective-permute-start.8 = (bf16[128,512]{1,0:T(8,128)(2,1)S(1)}, bf16[128,512]{1,0:T(8,128)(2,1)S(1)}, u32[]{:S(2)}, u32[]{:S(2)}) collective-permute-start(bf16[128,512]{1,0:T(8,128)(2,1)S(1)} %bitcast.43), channel_id=1, source_target_pairs={{0,3},{1,0},{2,1},{3,2},{4,7},{5,4},{6,5},{7,6},{8,11},{9,8},{10,9... | collective-permute-start | bytes 393224 | tf_op jit(solution)/shard_map/ppermute | solution.py:34
  126.2 5.1 %collective-permute-start.4 = (bf16[128,512]{1,0:T(8,128)(2,1)S(1)}, bf16[128,512]{1,0:T(8,128)(2,1)S(1)}, u32[]{:S(2)}, u32[]{:S(2)}) collective-permute-start(bf16[128,512]{1,0:T(8,128)(2,1)S(1)} %bitcast.44), channel_id=1, source_target_pairs={{0,1},{1,2},{2,3},{3,0},{4,5},{5,6},{6,7},{7,4},{8,9},{9,10},{10,1... | collective-permute-start | bytes 393224 | tf_op jit(solution)/shard_map/ppermute | solution.py:34
  131.3 1.9 %collective-permute-start.6 = (bf16[128,512]{1,0:T(8,128)(2,1)S(1)}, bf16[128,512]{1,0:T(8,128)(2,1)S(1)}, u32[]{:S(2)}, u32[]{:S(2)}) collective-permute-start(bf16[128,512]{1,0:T(8,128)(2,1)S(1)} %bitcast.45), channel_id=1, source_target_pairs={{0,2},{1,3},{2,0},{3,1},{4,6},{5,7},{6,4},{7,5},{8,10},{9,11},{10,... | collective-permute-start | bytes 393224 | tf_op jit(solution)/shard_map/ppermute | solution.py:34
  133.2 2.8 %collective-permute-start.7 = (bf16[128,1344]{1,0:T(8,128)(2,1)S(1)}, bf16[128,1344]{1,0:T(8,128)(2,1)S(1)}, u32[]{:S(2)}, u32[]{:S(2)}) collective-permute-start(bf16[128,1344]{1,0:T(8,128)(2,1)S(1)} %bitcast.34), channel_id=1, source_target_pairs={{0,3},{1,0},{2,1},{3,2},{4,7},{5,4},{6,5},{7,6},{8,11},{9,8},{10,9... | collective-permute-start | bytes 1032200 | tf_op jit(solution)/shard_map/ppermute | solution.py:34
  136.0 0.3 fusion.9
  136.3 1.1 collective-permute-done.4
  137.4 3.5 %collective-permute-start.5 = (bf16[128,1344]{1,0:T(8,128)(2,1)S(1)}, bf16[128,1344]{1,0:T(8,128)(2,1)S(1)}, u32[]{:S(2)}, u32[]{:S(2)}) collective-permute-start(bf16[128,1344]{1,0:T(8,128)(2,1)S(1)} %bitcast.36), channel_id=1, source_target_pairs={{0,2},{1,3},{2,0},{3,1},{4,6},{5,7},{6,4},{7,5},{8,10},{9,11},{10,... | collective-permute-start | bytes 1032200 | tf_op jit(solution)/shard_map/ppermute | solution.py:34
  140.9 0.0 collective-permute-done.3
  140.9 0.3 convolution_add_fusion.3
  141.2 0.0 collective-permute-done.8
  141.2 7.0 %collective-permute-done.7 = bf16[128,1344]{1,0:T(8,128)(2,1)S(1)} collective-permute-done((bf16[128,1344]{1,0:T(8,128)(2,1)S(1)}, bf16[128,1344]{1,0:T(8,128)(2,1)S(1)}, u32[]{:S(2)}, u32[]{:S(2)}) %collective-permute-start.7) | collective-permute-done | bytes 344096 | tf_op jit(solution)/shard_map/ppermute | solution.py:34
  148.2 0.3 fusion.5
  148.5 0.0 collective-permute-done.6
  148.5 6.5 %collective-permute-done.5 = bf16[128,1344]{1,0:T(8,128)(2,1)S(1)} collective-permute-done((bf16[128,1344]{1,0:T(8,128)(2,1)S(1)}, bf16[128,1344]{1,0:T(8,128)(2,1)S(1)}, u32[]{:S(2)}, u32[]{:S(2)}) %collective-permute-start.5) | collective-permute-done | bytes 344096 | tf_op jit(solution)/shard_map/ppermute | solution.py:34
  155.0 0.3 fusion.4
  155.3 0.2 fusion.15
  155.5 0.2 fusion.11
  155.7 0.2 convolution_add_fusion.1
  155.9 0.2 fusion.2
  156.2 1.3 copy.18
  (6 shorter events, 0.1 us)
Async XLA Ops:
  25.9 13.5 %copy-start = (f32[1,42,1024]{2,0,1:T(1,128)S(1)}, f32[1,42,1024]{2,0,1:T(1,128)}, u32[]{:S(2)}) copy-start(f32[1,42,1024]{2,0,1:T(1,128)} %param.10) | copy-start | bytes 516100
  26.8 47.3 %copy-start.1 = (bf16[1,32,512]{2,1,0:T(8,128)(2,1)S(1)}, bf16[1,32,512]{2,1,0:T(8,128)(2,1)}, u32[]{:S(2)}) copy-start(bf16[1,32,512]{2,1,0:T(8,128)(2,1)} %param.11) | copy-start | bytes 98308
  26.8 32.1 %all-to-all-start.1 = ((bf16[4,42,1024]{2,1,0:T(8,128)(2,1)}), bf16[4,42,1024]{2,1,0:T(8,128)(2,1)S(1)}, u32[]{:S(2)}, u32[]{:S(2)}) async-start(bf16[4,42,1024]{2,1,0:T(8,128)(2,1)} %sum_over_x.1), calls=%async_computation.1 | async-start | bytes 786432 | tf_op jit(solution)/shard_map/all_to_all | solution.py:26
  61.8 35.5 %all-to-all-start.2 = ((bf16[32,2,672]{2,1,0:T(2,128)(2,1)}), bf16[32,2,672]{2,1,0:T(2,128)(2,1)S(1)}, u32[]{:S(2)}, u32[]{:S(2)}) async-start(bf16[32,2,672]{2,1,0:T(2,128)(2,1)} %reshape.24), calls=%async_computation.2 | async-start | bytes 196608 | tf_op jit(solution)/shard_map/all_to_all | solution.py:142
  74.4 15.1 %collective-permute-start.2 = (bf16[32,512]{1,0:T(8,128)(2,1)S(1)}, bf16[32,512]{1,0:T(8,128)(2,1)S(1)}, u32[]{:S(2)}, u32[]{:S(2)}) collective-permute-start(bf16[32,512]{1,0:T(8,128)(2,1)S(1)} %reshape.22), channel_id=1, source_target_pairs={{0,12},{4,0},{8,4},{12,8},{1,13},{5,1},{9,5},{13,9},{2,14},{6,2},{... | collective-permute-start | bytes 98312 | tf_op jit(solution)/shard_map/ppermute | solution.py:34
  79.5 14.5 %collective-permute-start.1 = (bf16[32,512]{1,0:T(8,128)(2,1)S(1)}, bf16[32,512]{1,0:T(8,128)(2,1)S(1)}, u32[]{:S(2)}, u32[]{:S(2)}) collective-permute-start(bf16[32,512]{1,0:T(8,128)(2,1)S(1)} %reshape.22), channel_id=1, source_target_pairs={{0,8},{4,12},{8,0},{12,4},{1,9},{5,13},{9,1},{13,5},{2,10},{6,14},... | collective-permute-start | bytes 98312 | tf_op jit(solution)/shard_map/ppermute | solution.py:34
  85.4 11.8 %collective-permute-start = (bf16[32,512]{1,0:T(8,128)(2,1)S(1)}, bf16[32,512]{1,0:T(8,128)(2,1)S(1)}, u32[]{:S(2)}, u32[]{:S(2)}) collective-permute-start(bf16[32,512]{1,0:T(8,128)(2,1)S(1)} %reshape.22), channel_id=1, source_target_pairs={{0,4},{4,8},{8,12},{12,0},{1,5},{5,9},{9,13},{13,1},{2,6},{6,10},{... | collective-permute-start | bytes 98312 | tf_op jit(solution)/shard_map/ppermute | solution.py:34
  120.2 20.6 %collective-permute-start.3 = (bf16[128,1344]{1,0:T(8,128)(2,1)S(1)}, bf16[128,1344]{1,0:T(8,128)(2,1)S(1)}, u32[]{:S(2)}, u32[]{:S(2)}) collective-permute-start(bf16[128,1344]{1,0:T(8,128)(2,1)S(1)} %bitcast.33), channel_id=1, source_target_pairs={{0,1},{1,2},{2,3},{3,0},{4,5},{5,6},{6,7},{7,4},{8,9},{9,10},{10,1... | collective-permute-start | bytes 1032200 | tf_op jit(solution)/shard_map/ppermute | solution.py:34
  124.2 16.9 %collective-permute-start.8 = (bf16[128,512]{1,0:T(8,128)(2,1)S(1)}, bf16[128,512]{1,0:T(8,128)(2,1)S(1)}, u32[]{:S(2)}, u32[]{:S(2)}) collective-permute-start(bf16[128,512]{1,0:T(8,128)(2,1)S(1)} %bitcast.43), channel_id=1, source_target_pairs={{0,3},{1,0},{2,1},{3,2},{4,7},{5,4},{6,5},{7,6},{8,11},{9,8},{10,9... | collective-permute-start | bytes 393224 | tf_op jit(solution)/shard_map/ppermute | solution.py:34
  126.2 11.3 %collective-permute-start.4 = (bf16[128,512]{1,0:T(8,128)(2,1)S(1)}, bf16[128,512]{1,0:T(8,128)(2,1)S(1)}, u32[]{:S(2)}, u32[]{:S(2)}) collective-permute-start(bf16[128,512]{1,0:T(8,128)(2,1)S(1)} %bitcast.44), channel_id=1, source_target_pairs={{0,1},{1,2},{2,3},{3,0},{4,5},{5,6},{6,7},{7,4},{8,9},{9,10},{10,1... | collective-permute-start | bytes 393224 | tf_op jit(solution)/shard_map/ppermute | solution.py:34
  131.3 17.2 %collective-permute-start.6 = (bf16[128,512]{1,0:T(8,128)(2,1)S(1)}, bf16[128,512]{1,0:T(8,128)(2,1)S(1)}, u32[]{:S(2)}, u32[]{:S(2)}) collective-permute-start(bf16[128,512]{1,0:T(8,128)(2,1)S(1)} %bitcast.45), channel_id=1, source_target_pairs={{0,2},{1,3},{2,0},{3,1},{4,6},{5,7},{6,4},{7,5},{8,10},{9,11},{10,... | collective-permute-start | bytes 393224 | tf_op jit(solution)/shard_map/ppermute | solution.py:34
  133.2 15.0 %collective-permute-start.7 = (bf16[128,1344]{1,0:T(8,128)(2,1)S(1)}, bf16[128,1344]{1,0:T(8,128)(2,1)S(1)}, u32[]{:S(2)}, u32[]{:S(2)}) collective-permute-start(bf16[128,1344]{1,0:T(8,128)(2,1)S(1)} %bitcast.34), channel_id=1, source_target_pairs={{0,3},{1,0},{2,1},{3,2},{4,7},{5,4},{6,5},{7,6},{8,11},{9,8},{10,9... | collective-permute-start | bytes 1032200 | tf_op jit(solution)/shard_map/ppermute | solution.py:34
  137.4 17.6 %collective-permute-start.5 = (bf16[128,1344]{1,0:T(8,128)(2,1)S(1)}, bf16[128,1344]{1,0:T(8,128)(2,1)S(1)}, u32[]{:S(2)}, u32[]{:S(2)}) collective-permute-start(bf16[128,1344]{1,0:T(8,128)(2,1)S(1)} %bitcast.36), channel_id=1, source_target_pairs={{0,2},{1,3},{2,0},{3,1},{4,6},{5,7},{6,4},{7,5},{8,10},{9,11},{10,... | collective-permute-start | bytes 1032200 | tf_op jit(solution)/shard_map/ppermute | solution.py:34
where the time goes:
time: 158 us; the launch traced here: 157 us
  starting transfers between devices  58.7 us (37%)
  blocking collectives  42.9 us (27%)
  waiting for transfers between devices  41.2 us (26%)
  Pallas kernels  6.08 us (4%)
  local copies, waits for them, and re-layouts  4.81 us (3%)
  matrix products  1.95 us (1%)
  between operations  1.67 us (1%)
    ppermute x9, starting transfers between devices, steps(): pieces.append(lax.ppermute(block, axis, ring))  33.9 us
    ppermute x9, waiting for transfers between devices, steps(): pieces.append(lax.ppermute(block, axis, ring))  22.3 us
    all_gather x1, blocking collectives, step(): cycle = lax.all_gather(local, 'zh', axis=0).reshape(nz * col_width, -1)  21.8 us
    all_to_all x1, blocking collectives, exchange(): return lax.all_to_all(blocks, axis, split_axis=0, concat_axis=0, tiled=True)  21.1 us
    all_to_all x1, waiting for transfers between devices, exchange(): return lax.all_to_all(blocks, axis, split_axis=0, concat_axis=0, tiled=True)  18.9 us
    all_to_all x1, starting transfers between devices, exchange(): return lax.all_to_all(blocks, axis, split_axis=0, concat_axis=0, tiled=True)  12.5 us
    all_to_all x1, starting transfers between devices, step(): lax.all_to_all(updated.reshape(rows_dev, tot_count, col_width), KTOT, spl...  12.3 us
    pallas_call x1, Pallas kernels, ladder_part(): pl.pallas_call(kernel, grid=(width // tn,), in_specs=[pl.BlockSpec((1, 1)...  3.47 us
  transfers between devices with their start and end apart: 11, of which 6 were waited for; matrix products, arithmetic and copies ran while one was open for 1% of the time, Pallas kernels for 0%

commit v1 on v0

--- a/solution.py
+++ b/solution.py
@@ -54,7 +54,7 @@
 
     def kernel(mark_ref, amp_ref, w_ref, out_ref):
         product = jnp.dot(amp_ref[...], w_ref[...], preferred_element_type=jnp.float32)
-        product = product * mark_ref[...].astype(jnp.float32)
+        product = product * mark_ref[0, 0].astype(jnp.float32)
         here = pl.ds(pl.multiple_of(pl.program_id(0) * tn, tn), tn)
         for x in range(nx):
             slabs = [product[(z * nx + x) * one : (z * nx + x + 1) * one] for z in range(nz)]
@@ -64,7 +64,7 @@
         kernel,
         grid=(width // tn,),
         in_specs=[
-            pl.BlockSpec((1, 1), lambda j: (0, 0)),
+            pl.BlockSpec(memory_space=pltpu.SMEM),
             pl.BlockSpec((rows, inner), lambda j: (0, 0)),
             pl.BlockSpec((inner, tn), lambda j: (0, j)),
         ],
@@ -75,48 +75,53 @@
     )(listed, amp, weights)
 
 
-def sum_over_x(got, nz):
+def sum_over_x(got, nz, me):
     nx, rows, width = got.shape
     one = rows // nz
     tn = columns_block(width)
 
-    def kernel(in_ref, out_ref):
+    def kernel(me_ref, in_ref, *refs):
+        out_refs, slabs = refs[:-1], refs[-1]
         for j in range(width // tn):
             here = slice(j * tn, (j + 1) * tn)
             total = in_ref[0, :, here].astype(jnp.float32)
             for x in range(1, nx):
                 total = total + in_ref[x, :, here].astype(jnp.float32)
             for z in range(nz):
-                out_ref[z, :, here] = total[z * one : (z + 1) * one].astype(jnp.bfloat16)
+                slabs[z, :, here] = total[z * one : (z + 1) * one].astype(jnp.bfloat16)
+        for s, out_ref in enumerate(out_refs):
+            out_ref[...] = slabs[lax.rem(me_ref[0] + s, nz)]
 
     return pl.pallas_call(
         kernel,
-        in_specs=[WHOLE],
-        out_specs=WHOLE,
-        out_shape=near_out((nz, one, width)),
+        in_specs=[pl.BlockSpec(memory_space=pltpu.SMEM), WHOLE],
+        out_specs=[WHOLE] * nz,
+        out_shape=[near_out((one, width))] * nz,
+        scratch_shapes=[pltpu.VMEM((nz, one, width), jnp.bfloat16)],
         interpret=INTERPRET,
         name="sum_over_x",
-    )(near(got))
+    )(me.reshape(1), near(got))
 
 
-def update(got, current, denominators):
-    nz, one, width = got.shape
+def update(parts, current, denominators):
+    one, width = current.shape
 
-    def kernel(in_ref, current_ref, den_ref, ladder_ref, updated_ref):
-        total = in_ref[0].astype(jnp.float32)
-        for z in range(1, nz):
-            total = total + in_ref[z].astype(jnp.float32)
+    def kernel(*refs):
+        in_refs, (current_ref, den_ref, ladder_ref, updated_ref) = refs[:-4], refs[-4:]
+        total = in_refs[0][...].astype(jnp.float32)
+        for in_ref in in_refs[1:]:
+            total = total + in_ref[...].astype(jnp.float32)
         ladder_ref[...] = total.astype(jnp.bfloat16)
         updated_ref[...] = (current_ref[...].astype(jnp.float32) + total / den_ref[...]).astype(jnp.bfloat16)
 
     return pl.pallas_call(
         kernel,
-        in_specs=[WHOLE] * 3,
+        in_specs=[WHOLE] * (len(parts) + 2),
         out_specs=[WHOLE] * 2,
-        out_shape=[jax.ShapeDtypeStruct((one, width), jnp.bfloat16), near_out((one, width))],
+        out_shape=[near_out((one, width))] * 2,
         interpret=INTERPRET,
         name="update",
-    )(near(got), current, denominators)
+    )(*map(near, (*parts, current, denominators)))
 
 
 def step(amplitudes, ladder_integrals, listed, current, denominators, cycle_integrals):
@@ -133,8 +138,11 @@
     got = exchange(part, "x")
     own = own.reshape(col_width, nz, nx, col_width).transpose(0, 2, 1, 3).reshape(col_width, cols)
     own_pieces = steps(own, "zh")
-    part = sum_over_x(got, nz)
-    got = exchange(part, "zh")
+    parts = sum_over_x(got, nz, lax.axis_index("zh"))
+    got = [parts[0]]
+    for step in range(1, nz):
+        ring = [(i, (i + step) % nz) for i in range(nz)]
+        got.append(lax.ppermute(parts[step], "zh", ring))
     ints = ordered(own_pieces, "zh").reshape(nz * col_width, cols)
     int_pieces = steps(ints, "x")
     ladder, updated = update(got, current[0], denominators[0])

time: 158 us -> 157 us (level)
  blocking collectives: 42.9 us -> 21.4 us
  starting transfers between devices: 58.7 us -> 77.3 us
  waiting for transfers between devices: 41.2 us -> 44 us
    ppermute x0 -> x3, starting transfers between devices: none -> 22.8 us  [step(): got.append(lax.ppermute(parts[step], 'zh', ring))]
    all_to_all x1 -> x0, blocking collectives: 21.1 us -> none  [exchange(): return lax.all_to_all(blocks, axis, split_axis=0, concat_axis=0, tiled=True)]
    ppermute x0 -> x3, waiting for transfers between devices: none -> 8.5 us  [step(): got.append(lax.ppermute(parts[step], 'zh', ring))]
    all_to_all x1, starting transfers between devices: 12.5 us -> 4.77 us  [exchange(): return lax.all_to_all(blocks, axis, split_axis=0, concat_axis=0, tiled=True)]
    ppermute x9, starting transfers between devices: 33.9 us -> 38.9 us  [steps(): pieces.append(lax.ppermute(block, axis, ring))]
    ppermute x9, waiting for transfers between devices: 22.3 us -> 19 us  [steps(): pieces.append(lax.ppermute(block, axis, ring))]
    all_to_all x1, waiting for transfers between devices: 18.9 us -> 16.5 us  [exchange(): return lax.all_to_all(blocks, axis, split_axis=0, concat_axis=0, tiled=True)]
    unnamed x8 -> x11, local copies, waits for them, and re-layouts: 3.4 us -> 3.37 us
  transfers between devices with their start and end apart: 11 -> 14, of which waited for: 6 -> 7; matrix products, arithmetic and copies ran while one was open for 1% -> 1% of each run, Pallas kernels for 0% -> 0%
where the time goes in v1:
time: 157 us; the launch traced here: 156 us
  starting transfers between devices  77.3 us (49%)
  waiting for transfers between devices  44 us (28%)
  blocking collectives  21.4 us (14%)
  Pallas kernels  4.92 us (3%)
  local copies, waits for them, and re-layouts  4.79 us (3%)
  matrix products  1.94 us (1%)
  between operations  1.74 us (1%)
    ppermute x9, starting transfers between devices, steps(): pieces.append(lax.ppermute(block, axis, ring))  38.9 us
    ppermute x3, starting transfers between devices, step(): got.append(lax.ppermute(parts[step], 'zh', ring))  22.8 us
    all_gather x1, blocking collectives, step(): cycle = lax.all_gather(local, 'zh', axis=0).reshape(nz * col_width, -1)  21.4 us
    ppermute x9, waiting for transfers between devices, steps(): pieces.append(lax.ppermute(block, axis, ring))  19 us
    all_to_all x1, waiting for transfers between devices, exchange(): return lax.all_to_all(blocks, axis, split_axis=0, concat_axis=0, tiled=True)  16.5 us
    all_to_all x1, starting transfers between devices, step(): lax.all_to_all(updated.reshape(rows_dev, tot_count, col_width), KTOT, spl...  10.9 us
    ppermute x3, waiting for transfers between devices, step(): got.append(lax.ppermute(parts[step], 'zh', ring))  8.5 us
    all_to_all x1, starting transfers between devices, exchange(): return lax.all_to_all(blocks, axis, split_axis=0, concat_axis=0, tiled=True)  4.77 us
  transfers between devices with their start and end apart: 14, of which 7 were waited for; matrix products, arithmetic and copies ran while one was open for 1% of the time, Pallas kernels for 0%

profile of v1, /device:TPU:102, one launch (start us, length us, event | category | flops | bytes accessed | tf_op | source)
XLA Modules:
  0.0 156.2 jit_solution(8009775446679866127)
XLA Ops:
  1.3 4.5 %ladder_part.1 = bf16[4,168,1024]{2,1,0:T(8,128)(2,1)} custom-call(s32[1,1]{1,0:T(1,128)S(6)} %copy.26.mark_ref, bf16[672,1024]{1,0:T(8,128)(2,1)} %bitcast.42, bf16[1024,1024]{1,0:T(8,128)(2,1)} %bitcast.36), custom_call_target="tpu_custom_call" | custom-call | tf_op jit(solution)/shard_map/ladder_part/pallas_call | solution.py:63
  5.8 4.8 %all-to-all-start = ((bf16[4,168,1024]{2,1,0:T(8,128)(2,1)}), bf16[4,168,1024]{2,1,0:T(8,128)(2,1)S(1)}, u32[]{:S(2)}, u32[]{:S(2)}) async-start(bf16[4,168,1024]{2,1,0:T(8,128)(2,1)} %ladder_part.1), calls=%async_computation | async-start | bytes 2752512 | tf_op jit(solution)/shard_map/all_to_all | solution.py:26
  10.6 16.5 %all-to-all-done.in_ref = bf16[4,168,1024]{2,1,0:T(8,128)(2,1)S(1)} async-done(((bf16[4,168,1024]{2,1,0:T(8,128)(2,1)}), bf16[4,168,1024]{2,1,0:T(8,128)(2,1)S(1)}, u32[]{:S(2)}, u32[]{:S(2)}) %all-to-all-start) | async-done | bytes 1376288 | tf_op jit(solution)/shard_map/all_to_all | solution.py:26
  27.1 0.3 sum_over_x.1
  27.4 9.1 %collective-permute-start = (bf16[42,1024]{1,0:T(8,128)(2,1)S(1)}, bf16[42,1024]{1,0:T(8,128)(2,1)S(1)}, u32[]{:S(2)}, u32[]{:S(2)}) collective-permute-start(bf16[42,1024]{1,0:T(8,128)(2,1)S(1)} %get-tuple-element.12), channel_id=1, source_target_pairs={{0,4},{4,8},{8,12},{12,0},{1,5},{5,9},{9,13},{13,1},{2,6},{6,10},{... | collective-permute-start | bytes 258056 | tf_op jit(solution)/shard_map/ppermute | solution.py:145
  36.5 8.2 %collective-permute-start.1 = (bf16[42,1024]{1,0:T(8,128)(2,1)S(1)}, bf16[42,1024]{1,0:T(8,128)(2,1)S(1)}, u32[]{:S(2)}, u32[]{:S(2)}) collective-permute-start(bf16[42,1024]{1,0:T(8,128)(2,1)S(1)} %get-tuple-element.13), channel_id=1, source_target_pairs={{0,8},{4,12},{8,0},{12,4},{1,9},{5,13},{9,1},{13,5},{2,10},{6,14},... | collective-permute-start | bytes 258056 | tf_op jit(solution)/shard_map/ppermute | solution.py:145
  44.8 5.5 %collective-permute-start.2 = (bf16[42,1024]{1,0:T(8,128)(2,1)S(1)}, bf16[42,1024]{1,0:T(8,128)(2,1)S(1)}, u32[]{:S(2)}, u32[]{:S(2)}) collective-permute-start(bf16[42,1024]{1,0:T(8,128)(2,1)S(1)} %get-tuple-element.14), channel_id=1, source_target_pairs={{0,12},{4,0},{8,4},{12,8},{1,13},{5,1},{9,5},{13,9},{2,14},{6,2},{... | collective-permute-start | bytes 258056 | tf_op jit(solution)/shard_map/ppermute | solution.py:145
  50.3 0.0 collective-permute-done.refs_1_
  50.3 8.5 %collective-permute-done.1.refs_2_ = bf16[42,1024]{1,0:T(8,128)(2,1)S(1)} collective-permute-done((bf16[42,1024]{1,0:T(8,128)(2,1)S(1)}, bf16[42,1024]{1,0:T(8,128)(2,1)S(1)}, u32[]{:S(2)}, u32[]{:S(2)}) %collective-permute-start.1) | collective-permute-done | bytes 86048 | tf_op jit(solution)/shard_map/ppermute | solution.py:145
  58.8 0.0 collective-permute-done.2.refs_3_
  58.8 0.1 update.1
  58.9 0.2 copy.19
  59.1 1.0 reshape.28
  60.1 10.9 %all-to-all-start.1 = ((bf16[32,2,672]{2,1,0:T(2,128)(2,1)}), bf16[32,2,672]{2,1,0:T(2,128)(2,1)S(1)}, u32[]{:S(2)}, u32[]{:S(2)}) async-start(bf16[32,2,672]{2,1,0:T(2,128)(2,1)} %reshape.28), calls=%async_computation.1 | async-start | bytes 196608 | tf_op jit(solution)/shard_map/all_to_all | solution.py:150
  71.0 0.1 reshape.25
  71.1 0.1 copy.24
  71.2 0.2 reshape.26
  71.4 5.6 %collective-permute-start.5 = (bf16[32,512]{1,0:T(8,128)(2,1)S(1)}, bf16[32,512]{1,0:T(8,128)(2,1)S(1)}, u32[]{:S(2)}, u32[]{:S(2)}) collective-permute-start(bf16[32,512]{1,0:T(8,128)(2,1)S(1)} %reshape.26), channel_id=1, source_target_pairs={{0,12},{4,0},{8,4},{12,8},{1,13},{5,1},{9,5},{13,9},{2,14},{6,2},{... | collective-permute-start | bytes 98312 | tf_op jit(solution)/shard_map/ppermute | solution.py:34
  76.9 8.8 %collective-permute-start.4 = (bf16[32,512]{1,0:T(8,128)(2,1)S(1)}, bf16[32,512]{1,0:T(8,128)(2,1)S(1)}, u32[]{:S(2)}, u32[]{:S(2)}) collective-permute-start(bf16[32,512]{1,0:T(8,128)(2,1)S(1)} %reshape.26), channel_id=1, source_target_pairs={{0,8},{4,12},{8,0},{12,4},{1,9},{5,13},{9,1},{13,5},{2,10},{6,14},... | collective-permute-start | bytes 98312 | tf_op jit(solution)/shard_map/ppermute | solution.py:34
  85.7 4.8 %collective-permute-start.3 = (bf16[32,512]{1,0:T(8,128)(2,1)S(1)}, bf16[32,512]{1,0:T(8,128)(2,1)S(1)}, u32[]{:S(2)}, u32[]{:S(2)}) collective-permute-start(bf16[32,512]{1,0:T(8,128)(2,1)S(1)} %reshape.26), channel_id=1, source_target_pairs={{0,4},{4,8},{8,12},{12,0},{1,5},{5,9},{9,13},{13,1},{2,6},{6,10},{... | collective-permute-start | bytes 98312 | tf_op jit(solution)/shard_map/ppermute | solution.py:34
  90.5 0.2 stack_reshape.3
  90.9 0.8 collective-permute-done.4
  91.7 4.6 %collective-permute-done.3 = bf16[32,512]{1,0:T(8,128)(2,1)S(1)} collective-permute-done((bf16[32,512]{1,0:T(8,128)(2,1)S(1)}, bf16[32,512]{1,0:T(8,128)(2,1)S(1)}, u32[]{:S(2)}, u32[]{:S(2)}) %collective-permute-start.3) | collective-permute-done | bytes 32800 | tf_op jit(solution)/shard_map/ppermute | solution.py:34
  96.3 0.0 all-to-all-done.1
  96.3 0.4 reshape.29
  96.8 0.4 copy.16
  97.2 0.3 all_gather_reshape.3
  97.5 21.4 %all_gather.3 = bf16[4,32,1344]{2,1,0:T(8,128)(2,1)S(1)} all-gather(bf16[1,32,1344]{2,1,0:T(8,128)(2,1)S(1)} %all_gather_reshape.3), channel_id=1, replica_groups=mesh['zl'=4,'y'=4,'core'=2,'zh'=4,'x'=4] {'zh'}, dimensions={0}, use_global_device_ids=true | all-gather | bytes 430080 | tf_op jit(solution)/shard_map/all_gather | solution.py:154
  118.9 4.0 %collective-permute-start.6 = (bf16[128,1344]{1,0:T(8,128)(2,1)S(1)}, bf16[128,1344]{1,0:T(8,128)(2,1)S(1)}, u32[]{:S(2)}, u32[]{:S(2)}) collective-permute-start(bf16[128,1344]{1,0:T(8,128)(2,1)S(1)} %bitcast.37), channel_id=1, source_target_pairs={{0,1},{1,2},{2,3},{3,0},{4,5},{5,6},{6,7},{7,4},{8,9},{9,10},{10,1... | collective-permute-start | bytes 1032200 | tf_op jit(solution)/shard_map/ppermute | solution.py:34
  122.9 1.9 %collective-permute-start.11 = (bf16[128,512]{1,0:T(8,128)(2,1)S(1)}, bf16[128,512]{1,0:T(8,128)(2,1)S(1)}, u32[]{:S(2)}, u32[]{:S(2)}) collective-permute-start(bf16[128,512]{1,0:T(8,128)(2,1)S(1)} %bitcast.46), channel_id=1, source_target_pairs={{0,3},{1,0},{2,1},{3,2},{4,7},{5,4},{6,5},{7,6},{8,11},{9,8},{10,9... | collective-permute-start | bytes 393224 | tf_op jit(solution)/shard_map/ppermute | solution.py:34
  124.8 5.1 %collective-permute-start.7 = (bf16[128,512]{1,0:T(8,128)(2,1)S(1)}, bf16[128,512]{1,0:T(8,128)(2,1)S(1)}, u32[]{:S(2)}, u32[]{:S(2)}) collective-permute-start(bf16[128,512]{1,0:T(8,128)(2,1)S(1)} %bitcast.47), channel_id=1, source_target_pairs={{0,1},{1,2},{2,3},{3,0},{4,5},{5,6},{6,7},{7,4},{8,9},{9,10},{10,1... | collective-permute-start | bytes 393224 | tf_op jit(solution)/shard_map/ppermute | solution.py:34
  130.0 1.9 %collective-permute-start.9 = (bf16[128,512]{1,0:T(8,128)(2,1)S(1)}, bf16[128,512]{1,0:T(8,128)(2,1)S(1)}, u32[]{:S(2)}, u32[]{:S(2)}) collective-permute-start(bf16[128,512]{1,0:T(8,128)(2,1)S(1)} %bitcast.48), channel_id=1, source_target_pairs={{0,2},{1,3},{2,0},{3,1},{4,6},{5,7},{6,4},{7,5},{8,10},{9,11},{10,... | collective-permute-start | bytes 393224 | tf_op jit(solution)/shard_map/ppermute | solution.py:34
  131.9 0.6 copy.25
  132.6 2.8 %collective-permute-start.10 = (bf16[128,1344]{1,0:T(8,128)(2,1)S(1)}, bf16[128,1344]{1,0:T(8,128)(2,1)S(1)}, u32[]{:S(2)}, u32[]{:S(2)}) collective-permute-start(bf16[128,1344]{1,0:T(8,128)(2,1)S(1)} %bitcast.38), channel_id=1, source_target_pairs={{0,3},{1,0},{2,1},{3,2},{4,7},{5,4},{6,5},{7,6},{8,11},{9,8},{10,9... | collective-permute-start | bytes 1032200 | tf_op jit(solution)/shard_map/ppermute | solution.py:34
  135.3 0.3 fusion.9
  135.6 0.6 collective-permute-done.7
  136.2 4.0 %collective-permute-start.8 = (bf16[128,1344]{1,0:T(8,128)(2,1)S(1)}, bf16[128,1344]{1,0:T(8,128)(2,1)S(1)}, u32[]{:S(2)}, u32[]{:S(2)}) collective-permute-start(bf16[128,1344]{1,0:T(8,128)(2,1)S(1)} %bitcast.40), channel_id=1, source_target_pairs={{0,2},{1,3},{2,0},{3,1},{4,6},{5,7},{6,4},{7,5},{8,10},{9,11},{10,... | collective-permute-start | bytes 1032200 | tf_op jit(solution)/shard_map/ppermute | solution.py:34
  140.2 0.3 convolution_add_fusion.3
  140.5 6.7 %collective-permute-done.10 = bf16[128,1344]{1,0:T(8,128)(2,1)S(1)} collective-permute-done((bf16[128,1344]{1,0:T(8,128)(2,1)S(1)}, bf16[128,1344]{1,0:T(8,128)(2,1)S(1)}, u32[]{:S(2)}, u32[]{:S(2)}) %collective-permute-start.10) | collective-permute-done | bytes 344096 | tf_op jit(solution)/shard_map/ppermute | solution.py:34
  147.2 0.3 fusion.5
  147.5 0.0 collective-permute-done.9
  147.5 6.3 %collective-permute-done.8 = bf16[128,1344]{1,0:T(8,128)(2,1)S(1)} collective-permute-done((bf16[128,1344]{1,0:T(8,128)(2,1)S(1)}, bf16[128,1344]{1,0:T(8,128)(2,1)S(1)}, u32[]{:S(2)}, u32[]{:S(2)}) %collective-permute-start.8) | collective-permute-done | bytes 344096 | tf_op jit(solution)/shard_map/ppermute | solution.py:34
  153.8 0.3 fusion.4
  154.1 0.2 fusion.15
  154.3 0.2 fusion.11
  154.5 0.2 convolution_add_fusion.1
  154.7 0.2 fusion.2
  155.0 1.3 copy.18
  (14 shorter events, 0.1 us)
Async XLA Ops:
  5.8 21.3 %all-to-all-start = ((bf16[4,168,1024]{2,1,0:T(8,128)(2,1)}), bf16[4,168,1024]{2,1,0:T(8,128)(2,1)S(1)}, u32[]{:S(2)}, u32[]{:S(2)}) async-start(bf16[4,168,1024]{2,1,0:T(8,128)(2,1)} %ladder_part.1), calls=%async_computation | async-start | bytes 2752512 | tf_op jit(solution)/shard_map/all_to_all | solution.py:26
  10.6 39.7 %copy-start.1 = (f32[1,42,1024]{2,0,1:T(1,128)S(1)}, f32[1,42,1024]{2,0,1:T(1,128)}, u32[]{:S(2)}) copy-start(f32[1,42,1024]{2,0,1:T(1,128)} %param.10) | copy-start | bytes 516100
  10.6 48.2 %copy-start = (bf16[1,42,1024]{2,1,0:T(8,128)(2,1)S(1)}, bf16[1,42,1024]{2,1,0:T(8,128)(2,1)}, u32[]{:S(2)}) copy-start(bf16[1,42,1024]{2,1,0:T(8,128)(2,1)} %param.9) | copy-start | bytes 258052
  27.1 43.9 %copy-start.2 = (bf16[1,32,512]{2,1,0:T(8,128)(2,1)S(1)}, bf16[1,32,512]{2,1,0:T(8,128)(2,1)}, u32[]{:S(2)}) copy-start(bf16[1,32,512]{2,1,0:T(8,128)(2,1)} %param.11) | copy-start | bytes 98308
  27.4 22.9 %collective-permute-start = (bf16[42,1024]{1,0:T(8,128)(2,1)S(1)}, bf16[42,1024]{1,0:T(8,128)(2,1)S(1)}, u32[]{:S(2)}, u32[]{:S(2)}) collective-permute-start(bf16[42,1024]{1,0:T(8,128)(2,1)S(1)} %get-tuple-element.12), channel_id=1, source_target_pairs={{0,4},{4,8},{8,12},{12,0},{1,5},{5,9},{9,13},{13,1},{2,6},{6,10},{... | collective-permute-start | bytes 258056 | tf_op jit(solution)/shard_map/ppermute | solution.py:145
  36.5 22.3 %collective-permute-start.1 = (bf16[42,1024]{1,0:T(8,128)(2,1)S(1)}, bf16[42,1024]{1,0:T(8,128)(2,1)S(1)}, u32[]{:S(2)}, u32[]{:S(2)}) collective-permute-start(bf16[42,1024]{1,0:T(8,128)(2,1)S(1)} %get-tuple-element.13), channel_id=1, source_target_pairs={{0,8},{4,12},{8,0},{12,4},{1,9},{5,13},{9,1},{13,5},{2,10},{6,14},... | collective-permute-start | bytes 258056 | tf_op jit(solution)/shard_map/ppermute | solution.py:145
  44.8 14.0 %collective-permute-start.2 = (bf16[42,1024]{1,0:T(8,128)(2,1)S(1)}, bf16[42,1024]{1,0:T(8,128)(2,1)S(1)}, u32[]{:S(2)}, u32[]{:S(2)}) collective-permute-start(bf16[42,1024]{1,0:T(8,128)(2,1)S(1)} %get-tuple-element.14), channel_id=1, source_target_pairs={{0,12},{4,0},{8,4},{12,8},{1,13},{5,1},{9,5},{13,9},{2,14},{6,2},{... | collective-permute-start | bytes 258056 | tf_op jit(solution)/shard_map/ppermute | solution.py:145
  60.1 36.2 %all-to-all-start.1 = ((bf16[32,2,672]{2,1,0:T(2,128)(2,1)}), bf16[32,2,672]{2,1,0:T(2,128)(2,1)S(1)}, u32[]{:S(2)}, u32[]{:S(2)}) async-start(bf16[32,2,672]{2,1,0:T(2,128)(2,1)} %reshape.28), calls=%async_computation.1 | async-start | bytes 196608 | tf_op jit(solution)/shard_map/all_to_all | solution.py:150
  71.4 19.5 %collective-permute-start.5 = (bf16[32,512]{1,0:T(8,128)(2,1)S(1)}, bf16[32,512]{1,0:T(8,128)(2,1)S(1)}, u32[]{:S(2)}, u32[]{:S(2)}) collective-permute-start(bf16[32,512]{1,0:T(8,128)(2,1)S(1)} %reshape.26), channel_id=1, source_target_pairs={{0,12},{4,0},{8,4},{12,8},{1,13},{5,1},{9,5},{13,9},{2,14},{6,2},{... | collective-permute-start | bytes 98312 | tf_op jit(solution)/shard_map/ppermute | solution.py:34
  76.9 14.8 %collective-permute-start.4 = (bf16[32,512]{1,0:T(8,128)(2,1)S(1)}, bf16[32,512]{1,0:T(8,128)(2,1)S(1)}, u32[]{:S(2)}, u32[]{:S(2)}) collective-permute-start(bf16[32,512]{1,0:T(8,128)(2,1)S(1)} %reshape.26), channel_id=1, source_target_pairs={{0,8},{4,12},{8,0},{12,4},{1,9},{5,13},{9,1},{13,5},{2,10},{6,14},... | collective-permute-start | bytes 98312 | tf_op jit(solution)/shard_map/ppermute | solution.py:34
  85.7 10.5 %collective-permute-start.3 = (bf16[32,512]{1,0:T(8,128)(2,1)S(1)}, bf16[32,512]{1,0:T(8,128)(2,1)S(1)}, u32[]{:S(2)}, u32[]{:S(2)}) collective-permute-start(bf16[32,512]{1,0:T(8,128)(2,1)S(1)} %reshape.26), channel_id=1, source_target_pairs={{0,4},{4,8},{8,12},{12,0},{1,5},{5,9},{9,13},{13,1},{2,6},{6,10},{... | collective-permute-start | bytes 98312 | tf_op jit(solution)/shard_map/ppermute | solution.py:34
  118.9 21.3 %collective-permute-start.6 = (bf16[128,1344]{1,0:T(8,128)(2,1)S(1)}, bf16[128,1344]{1,0:T(8,128)(2,1)S(1)}, u32[]{:S(2)}, u32[]{:S(2)}) collective-permute-start(bf16[128,1344]{1,0:T(8,128)(2,1)S(1)} %bitcast.37), channel_id=1, source_target_pairs={{0,1},{1,2},{2,3},{3,0},{4,5},{5,6},{6,7},{7,4},{8,9},{9,10},{10,1... | collective-permute-start | bytes 1032200 | tf_op jit(solution)/shard_map/ppermute | solution.py:34
  122.9 17.6 %collective-permute-start.11 = (bf16[128,512]{1,0:T(8,128)(2,1)S(1)}, bf16[128,512]{1,0:T(8,128)(2,1)S(1)}, u32[]{:S(2)}, u32[]{:S(2)}) collective-permute-start(bf16[128,512]{1,0:T(8,128)(2,1)S(1)} %bitcast.46), channel_id=1, source_target_pairs={{0,3},{1,0},{2,1},{3,2},{4,7},{5,4},{6,5},{7,6},{8,11},{9,8},{10,9... | collective-permute-start | bytes 393224 | tf_op jit(solution)/shard_map/ppermute | solution.py:34
  124.8 11.3 %collective-permute-start.7 = (bf16[128,512]{1,0:T(8,128)(2,1)S(1)}, bf16[128,512]{1,0:T(8,128)(2,1)S(1)}, u32[]{:S(2)}, u32[]{:S(2)}) collective-permute-start(bf16[128,512]{1,0:T(8,128)(2,1)S(1)} %bitcast.47), channel_id=1, source_target_pairs={{0,1},{1,2},{2,3},{3,0},{4,5},{5,6},{6,7},{7,4},{8,9},{9,10},{10,1... | collective-permute-start | bytes 393224 | tf_op jit(solution)/shard_map/ppermute | solution.py:34
  130.0 17.5 %collective-permute-start.9 = (bf16[128,512]{1,0:T(8,128)(2,1)S(1)}, bf16[128,512]{1,0:T(8,128)(2,1)S(1)}, u32[]{:S(2)}, u32[]{:S(2)}) collective-permute-start(bf16[128,512]{1,0:T(8,128)(2,1)S(1)} %bitcast.48), channel_id=1, source_target_pairs={{0,2},{1,3},{2,0},{3,1},{4,6},{5,7},{6,4},{7,5},{8,10},{9,11},{10,... | collective-permute-start | bytes 393224 | tf_op jit(solution)/shard_map/ppermute | solution.py:34
  132.6 14.7 %collective-permute-start.10 = (bf16[128,1344]{1,0:T(8,128)(2,1)S(1)}, bf16[128,1344]{1,0:T(8,128)(2,1)S(1)}, u32[]{:S(2)}, u32[]{:S(2)}) collective-permute-start(bf16[128,1344]{1,0:T(8,128)(2,1)S(1)} %bitcast.38), channel_id=1, source_target_pairs={{0,3},{1,0},{2,1},{3,2},{4,7},{5,4},{6,5},{7,6},{8,11},{9,8},{10,9... | collective-permute-start | bytes 1032200 | tf_op jit(solution)/shard_map/ppermute | solution.py:34
  136.2 17.6 %collective-permute-start.8 = (bf16[128,1344]{1,0:T(8,128)(2,1)S(1)}, bf16[128,1344]{1,0:T(8,128)(2,1)S(1)}, u32[]{:S(2)}, u32[]{:S(2)}) collective-permute-start(bf16[128,1344]{1,0:T(8,128)(2,1)S(1)} %bitcast.40), channel_id=1, source_target_pairs={{0,2},{1,3},{2,0},{3,1},{4,6},{5,7},{6,4},{7,5},{8,10},{9,11},{10,... | collective-permute-start | bytes 1032200 | tf_op jit(solution)/shard_map/ppermute | solution.py:34
